TPU v7x, 512 devices: a whole 4x4x16 slice. The times are simulated.
512 devices in a mesh: tok: 32 (over y, x, core), voc: 16 (over z).
Axes of the slice: x: 4, y: 4, z: 16, core: 2. Of those that a mesh axis runs over, the one named last changes fastest.
Arguments:
- student_hidden: bfloat16 [512, 2560], P('tok', 'voc'), may hold values from -72 to 72
- teacher_rows: bfloat16 [512, 4096], P('tok', 'voc'), may hold values from -72 to 72
- student_head: bfloat16 [2560, 131072], P(None, ('tok', 'voc')), may hold values from -0.375 to 0.375
- teacher_head: bfloat16 [4096, 131072], P(None, ('tok', 'voc')), may hold values from -0.25 to 0.25
- lengths: int32 [32], replicated, may hold values from 1 to 16, 320 in all
- route: int32 [512], replicated, may hold values from 0 to 511, each once
- sampled_ids: int32 [512], replicated, may hold values from 0 to 131071
- mix_flags: int32 [512], replicated, may hold values 0 or 1
Outputs:
- divergence: float32 [512], P('tok')
- head_grad: bfloat16 [2560, 131072], P(None, ('tok', 'voc'))
Inputs may be any that keep to these rules, and one draw needn't show every extreme that they name: The lengths sum to 320; the largest is exactly 16. `route`: each trainer position appears once.
All inputs are finite; a program needn't handle non-finite values.
Results may differ from a plain program's by a relative error of at most 0.0052.
Values may be sent and summed in bfloat16 or wider, within the bound.
No kernel may reach another device: no remote copies, remote signals or barrier semaphores. Data moves between devices by JAX's collectives and lax.ppermute only.
A program may use at most 64 MiB of HBM per device.

v0:
```python
import jax
import jax.numpy as jnp
from jax import lax
from jax.sharding import PartitionSpec as P


def on_device(
    student_hidden, teacher_rows, student_head, teacher_head, lengths, route, sampled_ids, mix_flags
):
    tok_count = lax.axis_size("tok")
    voc_count = lax.axis_size("voc")
    group = lax.axis_index("tok")
    grp_rows = student_hidden.shape[0]
    vocab_dev = student_head.shape[1]
    first_col = (group * voc_count + lax.axis_index("voc")) * vocab_dev
    local_s, local_t = (student_hidden, teacher_rows)
    trainer_of = jnp.arange(grp_rows * tok_count, dtype=jnp.int32)
    live_rows = (trainer_of % grp_rows < lengths[trainer_of // grp_rows]).astype(jnp.float32)
    full_s, full_t = (
        lax.all_gather(local_s, "voc", axis=1, tiled=True),
        lax.all_gather(local_t, "voc", axis=1, tiled=True),
    )
    rows_s = lax.all_gather(full_s, "tok", axis=0, tiled=True)
    gathered = jnp.dot(
        lax.all_gather(full_t, "tok", axis=0, tiled=True),
        teacher_head,
        preferred_element_type=jnp.float32,
    )
    inverse = jnp.zeros_like(route).at[route].set(jnp.arange(route.shape[0], dtype=jnp.int32))
    teacher_logits = gathered[inverse]
    student_logits = jnp.dot(rows_s, student_head, preferred_element_type=jnp.float32)
    row_ids = sampled_ids[trainer_of]
    row_flags = mix_flags[trainer_of]
    onehot = row_ids[:, None] - first_col == jnp.arange(vocab_dev, dtype=jnp.int32)[None, :]
    pick_s = jnp.sum(jnp.where(onehot, student_logits, 0.0), axis=1)
    pick_u = jnp.sum(jnp.where(onehot, teacher_logits, 0.0), axis=1)
    s_max, u_max = lax.pmax(
        (jnp.max(student_logits, axis=1), jnp.max(teacher_logits, axis=1)), ("tok", "voc")
    )
    s_sum = jnp.sum(jnp.exp(student_logits - s_max[:, None]), axis=1)
    u_sum = jnp.sum(jnp.exp(teacher_logits - u_max[:, None]), axis=1)
    s_tot, u_tot, pick_s, pick_u = lax.psum((s_sum, u_sum, pick_s, pick_u), ("tok", "voc"))
    lse_s = s_max + jnp.log(s_tot)
    lse_u = u_max + jnp.log(u_tot)
    log_student = student_logits - lse_s[:, None]
    log_teacher = teacher_logits - lse_u[:, None]
    probs = jnp.exp(log_student)
    gap = log_student - log_teacher
    kl_all = lax.psum(jnp.sum(probs * gap, axis=1), ("tok", "voc"))
    mixed = 1.0 / (0.2 * jnp.exp(pick_u - lse_u - (pick_s - lse_s)) + 0.8)
    weight = jnp.where(row_flags == 1, mixed, jnp.ones_like(mixed))
    dlogits = ((live_rows * weight)[:, None] * probs * (gap - kl_all[:, None])).astype(jnp.bfloat16)
    head_grad = lax.dot_general(
        rows_s, dlogits, (((0,), (0,)), ((), ())), preferred_element_type=jnp.float32
    )
    kl_rows = live_rows * kl_all
    divergence = lax.dynamic_slice_in_dim(kl_rows, group * grp_rows, grp_rows)
    return (divergence, head_grad.astype(jnp.bfloat16))


def solution(mesh):
    in_specs = (
        P("tok", "voc"),
        P("tok", "voc"),
        P(None, ("tok", "voc")),
        P(None, ("tok", "voc")),
        P(),
        P(),
        P(),
        P(),
    )
    out_specs = (P("tok"), P(None, ("tok", "voc")))
    return jax.shard_map(
        on_device, mesh=mesh, in_specs=in_specs, out_specs=out_specs, check_vma=False
    )
```

profile of v0, /device:TPU:1, one launch (start us, length us, event | category | flops | bytes accessed | tf_op | source)
XLA Modules:
  0.0 505.5 jit_solution(3653330909238869689)
XLA Ops:
  7.2 0.0 copy-start
  7.2 0.0 copy-start.1
  7.2 0.0 copy-start.4
  7.2 0.0 all-gather.4.cloned.1.call-start
  7.2 0.0 copy-start.3
  7.3 30.2 %all-gather = bf16[16,160,16]{1,2,0:T(8,128)(2,1)S(1)} all-gather(bf16[1,160,16]{1,2,0:T(8,128)(2,1)} %bitcast.47), channel_id=1, replica_groups=mesh['tok'=32,'voc'=16] {'voc'}, dimensions={0}, use_global_device_ids=true | all-gather | bytes 87040 | tf_op jit(solution)/shard_map/all_gather | solution.py:20
  37.5 0.8 reshape.200
  38.3 0.0 all-gather.4.cloned.1.call-update
  38.4 0.0 all-gather.6.cloned.1.call-start
  38.4 22.4 %all_gather.14 = bf16[16,4096]{1,0:T(8,128)(2,1)} all-gather(bf16[16,256]{1,0:T(8,128)(2,1)} %param.9), channel_id=1, replica_groups=mesh['tok'=32,'voc'=16] {'voc'}, dimensions={1}, use_global_device_ids=true | all-gather | bytes 139264 | tf_op jit(solution)/shard_map/all_gather | solution.py:21
  60.8 0.0 all-gather.6.cloned.1.call-update
  60.8 3.6 gather_fusion.2
  64.4 0.0 copy-done.1
  64.4 3.5 gather_fusion.1
  67.9 0.0 copy-done.4
  68.0 2.4 scatter_custom_fusion
  71.3 0.0 copy-done.3
  71.3 0.7 fusion.14
  72.0 4.3 compare_select_fusion.1
  76.4 0.7 fusion.13
  77.1 24.5 %all-gather.4.cloned.1.call-done = bf16[512,2560]{1,0:T(8,128)(2,1)} async-done(((bf16[16,2560]{1,0:T(8,128)(2,1)}), bf16[512,2560]{1,0:T(8,128)(2,1)}) %all-gather.4.cloned.1.call-update) | async-done | bytes 2621456 | tf_op jit(solution)/shard_map/all_gather | solution.py:23
  101.6 3.8 fusion.15
  105.4 60.2 %all-gather.6.cloned.1.call-done = bf16[512,4096]{1,0:T(8,128)(2,1)} async-done(((bf16[16,4096]{1,0:T(8,128)(2,1)}), bf16[512,4096]{1,0:T(8,128)(2,1)}) %all-gather.6.cloned.1.call-update) | async-done | bytes 4194320 | tf_op jit(solution)/shard_map/all_gather | solution.py:25
  165.6 0.0 copy-done
  165.6 3.4 fusion.16
  169.1 1.6 gather_fusion
  170.7 0.0 copy-start.2
  170.7 1.0 copy.18
  171.7 0.1 reduce_max.19
  171.8 103.7 %all-reduce.2 = (f32[512]{0:T(512)S(1)}, f32[512]{0:T(512)S(1)}) all-reduce(f32[512]{0:T(512)S(1)} %reduce_max.19, f32[512]{0:T(512)S(1)} %get-tuple-element.52), channel_id=1, replica_groups=mesh['tok'=32,'voc'=16] {'tok','voc'}, use_global_device_ids=true, to_apply=%region_6.7 | all-reduce | flops 1024 | bytes 8192 | tf_op jit(solution)/shard_map/pmax | solution.py:37
  275.5 0.2 exponential_reduce_fusion
  275.7 1.2 exponential_reduce_fusion.1
  276.9 100.3 %all-reduce.1 = (f32[512]{0:T(512)S(1)}, f32[512]{0:T(512)S(1)}) all-reduce(f32[512]{0:T(512)S(1)} %exponential_reduce_fusion, f32[512]{0:T(512)S(1)} %exponential_reduce_fusion.1), channel_id=1, replica_groups=mesh['tok'=32,'voc'=16] {'tok','voc'}, use_global_device_ids=true, to_apply=%region_8.9 | all-reduce | flops 1024 | bytes 8192 | tf_op jit(solution)/shard_map/psum | solution.py:42
  377.2 0.0 copy-done.2
  377.2 1.3 select_reduce_fusion.1
  378.5 99.5 %all-reduce = (f32[512]{0:T(512)S(1)}, f32[512]{0:T(512)S(1)}, f32[512]{0:T(512)S(1)}) all-reduce(f32[512]{0:T(512)S(1)} %get-tuple-element.9, f32[512]{0:T(512)S(1)} %get-tuple-element.10, f32[512]{0:T(512)S(1)} %get-tuple-element.8), channel_id=1, replica_groups=mesh['tok'=32,'voc'=16] {'tok','voc'}, use_global_device_ids=true, to_apply=%region_10.11 | all-reduce | flops 1536 | bytes 12288 | tf_op jit(solution)/shard_map/psum | solution.py:49
  478.0 15.7 %fusion.5 = (f32[512]{0:T(512)S(1)}, pred[512]{0:T(512)(128)(4,1)S(1)}) fusion(f32[512]{0:T(512)S(1)} %get-tuple-element.12, f32[512]{0:T(512)S(1)} %get-tuple-element.55, f32[512]{0:T(512)S(1)} %get-tuple-element.13, f32[512]{0:T(512)S(1)} %get-tuple-element.54, s32[512]{0:T(512)S(1)} %gather_fusion.1, pred[512]{0:T(512)(128)(4,1)S(1)} %compare_reduce_fusion, ...), kind=kLoop, calls=%fused_computation.60 | loop fusion | flops 20992 | bytes 27748 | tf_op jit(solution)/shard_map/mul | solution.py:52
  493.7 2.9 fusion
  496.7 1.4 copy.20
  498.1 0.6 dynamic_slice.3
  (35 shorter events, 0.9 us)
Async XLA Ops:
  7.2 158.5 %copy-start = (bf16[4096,256]{1,0:T(8,128)(2,1)S(1)}, bf16[4096,256]{1,0:T(8,128)(2,1)}, u32[]{:S(2)}) copy-start(bf16[4096,256]{1,0:T(8,128)(2,1)} %param.11) | copy-start | bytes 6291460
  7.2 57.3 %copy-start.1 = (s32[512]{0:T(512)S(1)}, s32[512]{0:T(512)}, u32[]{:S(2)}) copy-start(s32[512]{0:T(512)} %param.15) | copy-start | bytes 6148
  7.2 60.8 %copy-start.4 = (s32[512]{0:T(512)S(1)}, s32[512]{0:T(512)}, u32[]{:S(2)}) copy-start(s32[512]{0:T(512)} %param.13) | copy-start | bytes 6148
  7.2 94.4 %all-gather.4.cloned.1.call-start = ((), (), s32[]{:S(2)}) async-start(), calls=%async_computation | async-start | bytes 2703360 | tf_op jit(solution)/shard_map/all_gather | solution.py:23
  7.2 64.0 %copy-start.3 = (s32[32]{0:T(128)S(1)}, s32[32]{0:T(128)}, u32[]{:S(2)}) copy-start(s32[32]{0:T(128)} %param.12) | copy-start | bytes 388
  38.4 127.3 %all-gather.6.cloned.1.call-start = ((), (), s32[]{:S(2)}) async-start(), calls=%async_computation.1 | async-start | bytes 4325376 | tf_op jit(solution)/shard_map/all_gather | solution.py:25
  170.7 206.5 %copy-start.2 = (f32[512,256]{0,1:T(8,128)S(1)}, f32[512,256]{0,1:T(8,128)}, u32[]{:S(2)}) copy-start(f32[512,256]{0,1:T(8,128)} %get-tuple-element.53) | copy-start | bytes 1572868
Sparse Core Ops, SparseCore 0:
  38.5 63.0 all-gather.3
  104.7 60.8 all-gather.5
where the time goes:
time: 506 us
  blocking collectives  356 us (70%)
  waiting for transfers between devices  84.7 us (17%)
  other arithmetic  23.8 us (5%)
  local copies, waits for them, and re-layouts  16.5 us (3%)
  between operations  14.2 us (3%)
  matrix products  10.2 us (2%)
    pmax x1, blocking collectives, on_device(): lax.pmax((jnp.max(student_logits, axis=1), jnp.max(teacher_logits, axis=1...  104 us
    psum x1, blocking collectives, on_device(): lax.psum((s_sum, u_sum, pick_s, pick_u), ('tok', 'voc'))  100 us
    psum x1, blocking collectives, on_device(): kl_all = lax.psum(jnp.sum(probs * gap, axis=1), ('tok', 'voc'))  99.5 us
    all_gather x1, waiting for transfers between devices, on_device(): lax.all_gather(full_t, 'tok', axis=0, tiled=True)  60.2 us
    all_gather x1, blocking collectives, on_device(): lax.all_gather(local_s, 'voc', axis=1, tiled=True)  30.2 us
    all_gather x1, waiting for transfers between devices, on_device(): rows_s = lax.all_gather(full_s, 'tok', axis=0, tiled=True)  24.5 us
    all_gather x1, blocking collectives, on_device(): lax.all_gather(local_t, 'voc', axis=1, tiled=True)  22.4 us
    mul x1, other arithmetic, on_device(): live_rows * weight  15.7 us
  transfers between devices with their start and end apart: 2, of which 2 were waited for; matrix products, arithmetic and copies ran while one was open for 4% of the time, Pallas kernels for 0%

commit v1 on v0

--- a/solution.py
+++ b/solution.py
@@ -21,10 +21,17 @@
         lax.all_gather(local_t, "voc", axis=1, tiled=True),
     )
     rows_s = lax.all_gather(full_s, "tok", axis=0, tiled=True)
+    remake_the_roads = lambda obj, axis_tag: jnp.concatenate(
+        lax.all_to_all(
+            jnp.stack([obj] * lax.psum(1, axis_name=axis_tag), axis=0),
+            axis_name=axis_tag,
+            split_axis=0,
+            concat_axis=0,
+        ),
+        axis=0,
+    )
     gathered = jnp.dot(
-        lax.all_gather(full_t, "tok", axis=0, tiled=True),
-        teacher_head,
-        preferred_element_type=jnp.float32,
+        remake_the_roads(full_t, "tok"), teacher_head, preferred_element_type=jnp.float32
     )
     inverse = jnp.zeros_like(route).at[route].set(jnp.arange(route.shape[0], dtype=jnp.int32))
     teacher_logits = gathered[inverse]

time: 506 us -> 479 us (0.947)
  waiting for transfers between devices: 84.7 us -> 38.7 us
  starting transfers between devices: 0.08 us -> 22 us
    all_gather x1 -> x0, waiting for transfers between devices: 60.2 us -> none  [on_device(): lax.all_gather(full_t, 'tok', axis=0, tiled=True)]
    all_to_all x0 -> x1, waiting for transfers between devices: none -> 38.6 us  [on_device(): lax.all_to_all(jnp.stack([obj] * lax.psum(1, axis_name=axis_tag), axis=0)...]
    all_gather x1, waiting for transfers between devices: 24.5 us -> 0.02 us  [on_device(): rows_s = lax.all_gather(full_s, 'tok', axis=0, tiled=True)]
    all_to_all x0 -> x1, starting transfers between devices: none -> 22 us  [on_device(): lax.all_to_all(jnp.stack([obj] * lax.psum(1, axis_name=axis_tag), axis=0)...]
  transfers between devices with their start and end apart: 2 -> 2, of which waited for: 2 -> 1; matrix products, arithmetic and copies ran while one was open for 4% -> 5% of each run, Pallas kernels for 0% -> 0%
where the time goes in v1:
time: 479 us; the launch traced here: 478 us
  blocking collectives  352 us (73%)
  waiting for transfers between devices  38.7 us (8%)
  other arithmetic  23.6 us (5%)
  starting transfers between devices  22 us (5%)
  local copies, waits for them, and re-layouts  18 us (4%)
  between operations  14.3 us (3%)
  matrix products  10.2 us (2%)
    pmax x1, blocking collectives, on_device(): lax.pmax((jnp.max(student_logits, axis=1), jnp.max(teacher_logits, axis=1...  102 us
    psum x1, blocking collectives, on_device(): kl_all = lax.psum(jnp.sum(probs * gap, axis=1), ('tok', 'voc'))  100 us
    psum x1, blocking collectives, on_device(): lax.psum((s_sum, u_sum, pick_s, pick_u), ('tok', 'voc'))  99.5 us
    all_to_all x1, waiting for transfers between devices, on_device(): lax.all_to_all(jnp.stack([obj] * lax.psum(1, axis_name=axis_tag), axis=0)...  38.6 us
    all_gather x1, blocking collectives, on_device(): lax.all_gather(local_s, 'voc', axis=1, tiled=True)  30.2 us
    all_to_all x1, starting transfers between devices, on_device(): lax.all_to_all(jnp.stack([obj] * lax.psum(1, axis_name=axis_tag), axis=0)...  22 us
    all_gather x1, blocking collectives, on_device(): lax.all_gather(local_t, 'voc', axis=1, tiled=True)  20 us
    mul x1, other arithmetic, on_device(): live_rows * weight  15.6 us
  transfers between devices with their start and end apart: 2, of which 1 were waited for; matrix products, arithmetic and copies ran while one was open for 5% of the time, Pallas kernels for 0%

profile of v1, /device:TPU:1, one launch (start us, length us, event | category | flops | bytes accessed | tf_op | source)
XLA Modules:
  0.0 478.3 jit_solution(2305605284519569021)
XLA Ops:
  7.2 0.0 copy-start
  7.2 0.0 all-gather.3.cloned.1.call-start
  7.2 30.2 %all-gather = bf16[16,160,16]{1,2,0:T(8,128)(2,1)S(1)} all-gather(bf16[1,160,16]{1,2,0:T(8,128)(2,1)} %bitcast.48), channel_id=1, replica_groups=mesh['tok'=32,'voc'=16] {'voc'}, dimensions={0}, use_global_device_ids=true | all-gather | bytes 87040 | tf_op jit(solution)/shard_map/all_gather | solution.py:20
  37.5 0.8 reshape.206
  38.3 0.0 all-gather.3.cloned.1.call-update
  38.3 20.0 %all_gather.11 = bf16[16,4096]{1,0:T(8,128)(2,1)S(1)} all-gather(bf16[16,256]{1,0:T(8,128)(2,1)} %param.9), channel_id=1, replica_groups=mesh['tok'=32,'voc'=16] {'voc'}, dimensions={1}, use_global_device_ids=true | all-gather | bytes 139264 | tf_op jit(solution)/shard_map/all_gather | solution.py:21
  58.3 2.5 stack.2
  60.8 0.0 copy-start.1
  60.8 22.0 %all-to-all-start = ((bf16[32,16,4096]{2,1,0:T(8,128)(2,1)}), bf16[32,16,4096]{2,1,0:T(8,128)(2,1)}, u32[]{:S(2)}, u32[]{:S(2)}) async-start(bf16[32,16,4096]{2,1,0:T(8,128)(2,1)} %stack.2), calls=%async_computation | async-start | bytes 8388608 | tf_op jit(solution)/shard_map/all_to_all | solution.py:25
  82.8 0.0 copy-start.2
  82.8 0.0 copy-start.5
  82.8 0.0 copy-start.4
  82.8 0.0 copy-done.1
  82.8 3.5 gather_fusion.2
  86.3 0.0 copy-done.2
  86.3 3.5 gather_fusion.1
  89.8 0.0 copy-done.5
  89.9 2.4 scatter_custom_fusion
  93.2 0.0 copy-done.4
  93.2 0.7 fusion.14
  93.9 4.3 compare_select_fusion.1
  98.2 0.7 fusion.13
  99.0 38.6 %all-to-all-done = bf16[32,16,4096]{2,1,0:T(8,128)(2,1)} async-done(((bf16[32,16,4096]{2,1,0:T(8,128)(2,1)}), bf16[32,16,4096]{2,1,0:T(8,128)(2,1)}, u32[]{:S(2)}, u32[]{:S(2)}) %all-to-all-start) | async-done | bytes 4194336 | tf_op jit(solution)/shard_map/all_to_all | solution.py:25
  137.6 0.0 copy-done
  137.6 3.4 fusion.16
  141.1 1.6 gather_fusion
  142.6 0.2 copy.18
  142.9 0.0 copy-start.3
  142.9 0.1 reduce_max.19
  143.0 0.0 all-gather.3.cloned.1.call-done
  143.0 3.8 fusion.15
  146.8 101.7 %all-reduce.2 = (f32[512]{0:T(512)S(1)}, f32[512]{0:T(512)S(1)}) all-reduce(f32[512]{0:T(512)S(1)} %reduce_max.19, f32[512]{0:T(512)S(1)} %get-tuple-element.52), channel_id=1, replica_groups=mesh['tok'=32,'voc'=16] {'tok','voc'}, use_global_device_ids=true, to_apply=%region_6.7 | all-reduce | flops 1024 | bytes 8192 | tf_op jit(solution)/shard_map/pmax | solution.py:44
  248.6 0.2 exponential_reduce_fusion
  248.8 1.2 exponential_reduce_fusion.1
  250.0 99.5 %all-reduce.1 = (f32[512]{0:T(512)S(1)}, f32[512]{0:T(512)S(1)}) all-reduce(f32[512]{0:T(512)S(1)} %exponential_reduce_fusion, f32[512]{0:T(512)S(1)} %exponential_reduce_fusion.1), channel_id=1, replica_groups=mesh['tok'=32,'voc'=16] {'tok','voc'}, use_global_device_ids=true, to_apply=%region_8.9 | all-reduce | flops 1024 | bytes 8192 | tf_op jit(solution)/shard_map/psum | solution.py:49
  349.5 0.0 copy-done.3
  349.5 1.3 select_reduce_fusion.1
  350.8 100.1 %all-reduce = (f32[512]{0:T(512)S(1)}, f32[512]{0:T(512)S(1)}, f32[512]{0:T(512)S(1)}) all-reduce(f32[512]{0:T(512)S(1)} %get-tuple-element.9, f32[512]{0:T(512)S(1)} %get-tuple-element.10, f32[512]{0:T(512)S(1)} %get-tuple-element.8), channel_id=1, replica_groups=mesh['tok'=32,'voc'=16] {'tok','voc'}, use_global_device_ids=true, to_apply=%region_10.11 | all-reduce | flops 1536 | bytes 12288 | tf_op jit(solution)/shard_map/psum | solution.py:56
  450.9 15.6 %fusion.5 = (f32[512]{0:T(512)S(1)}, pred[512]{0:T(512)(128)(4,1)S(1)}) fusion(f32[512]{0:T(512)S(1)} %get-tuple-element.12, f32[512]{0:T(512)S(1)} %get-tuple-element.55, f32[512]{0:T(512)S(1)} %get-tuple-element.13, f32[512]{0:T(512)S(1)} %get-tuple-element.54, s32[512]{0:T(512)S(1)} %gather_fusion.1, pred[512]{0:T(512)(128)(4,1)S(1)} %compare_reduce_fusion, ...), kind=kLoop, calls=%fused_computation.60 | loop fusion | flops 20992 | bytes 27748 | tf_op jit(solution)/shard_map/mul | solution.py:59
  466.5 2.9 fusion
  469.5 1.4 copy.20
  470.9 0.6 dynamic_slice.3
  (35 shorter events, 0.9 us)
Async XLA Ops:
  7.2 130.5 %copy-start = (bf16[4096,256]{1,0:T(8,128)(2,1)S(1)}, bf16[4096,256]{1,0:T(8,128)(2,1)}, u32[]{:S(2)}) copy-start(bf16[4096,256]{1,0:T(8,128)(2,1)} %param.11) | copy-start | bytes 6291460
  7.2 135.9 %all-gather.3.cloned.1.call-start = ((), (), s32[]{:S(2)}) async-start(), calls=%async_computation.1 | async-start | bytes 2703360 | tf_op jit(solution)/shard_map/all_gather | solution.py:23
  60.8 22.1 %copy-start.1 = (s32[512]{0:T(512)S(1)}, s32[512]{0:T(512)}, u32[]{:S(2)}) copy-start(s32[512]{0:T(512)} %param.14) | copy-start | bytes 6148
  60.8 76.9 %all-to-all-start = ((bf16[32,16,4096]{2,1,0:T(8,128)(2,1)}), bf16[32,16,4096]{2,1,0:T(8,128)(2,1)}, u32[]{:S(2)}, u32[]{:S(2)}) async-start(bf16[32,16,4096]{2,1,0:T(8,128)(2,1)} %stack.2), calls=%async_computation | async-start | bytes 8388608 | tf_op jit(solution)/shard_map/all_to_all | solution.py:25
  82.8 3.6 copy-start.2
  82.8 7.1 %copy-start.5 = (s32[512]{0:T(512)S(1)}, s32[512]{0:T(512)}, u32[]{:S(2)}) copy-start(s32[512]{0:T(512)} %param.13) | copy-start | bytes 6148
  82.8 10.4 %copy-start.4 = (s32[32]{0:T(128)S(1)}, s32[32]{0:T(128)}, u32[]{:S(2)}) copy-start(s32[32]{0:T(128)} %param.12) | copy-start | bytes 388
  142.9 206.7 %copy-start.3 = (f32[512,256]{0,1:T(8,128)}, f32[512,256]{0,1:T(8,128)S(1)}, u32[]{:S(2)}) copy-start(f32[512,256]{0,1:T(8,128)S(1)} %copy.18) | copy-start | bytes 1572868
Sparse Core Ops, SparseCore 0:
  38.4 97.1 all-gather.2
